TPU v7x, 32 devices: a whole 2x2x4 slice. The times are simulated.
32 devices in a mesh: rep: 1, ep: 32 (over z, y, x, core), hid: 1.
Axes of the slice: x: 2, y: 2, z: 4, core: 2. Of those that a mesh axis runs over, the one named last changes fastest.
Arguments:
- tokens: bfloat16 [4096, 2048], P(('rep', 'ep')), may hold values from -6 to 6
- cotangent: bfloat16 [4096, 2048], P(('rep', 'ep')), may hold values from -2 to 2
- routing: float32 [4096, 8], P(('rep', 'ep')), may hold values from 0.05 to 0.5
- expert_ids: int32 [4096, 8], P(('rep', 'ep')), may hold values from 0 to 63, all different within a row; in each aligned block of 128 rows (0 to 127, 128 to 255, ...) at most 20 rows name the same one
- gate_weight: bfloat16 [64, 2048, 768], P('ep', None, 'hid'), may hold values from -0.125 to 0.125
- up_weight: bfloat16 [64, 2048, 768], P('ep', None, 'hid'), may hold values from -0.125 to 0.125
- down_weight: bfloat16 [64, 768, 2048], P('ep', 'hid'), may hold values from -0.21875 to 0.21875
Outputs:
- input_grad: float32 [4096, 2048], P(('rep', 'ep'), 'hid')
- gate_grad: float32 [4096, 8], P(('rep', 'ep'))
Inputs may be any that keep to these rules, and one draw needn't show every extreme that they name: `expert_ids`: among the 128 tokens of one index of ep (aligned blocks of rows), no expert is picked more than 20 times, a bound that some block reaches; the 8 picks of a token are different experts.
All inputs are finite; a program needn't handle non-finite values.
Results may differ from a plain program's by a relative error of at most 0.0029.
Values may be sent and summed in bfloat16 or wider, within the bound.
A program may use at most 128 MiB of HBM per device.

v0:
```python
import functools

import jax
import jax.numpy as jnp
from jax import lax
from jax.experimental import pallas as pl
from jax.experimental.pallas import tpu as pltpu
from jax.sharding import PartitionSpec as P

BF = jnp.bfloat16
F32 = jnp.float32
PLANE = 8
LANES = 128
COLUMNS = 256


def dot(a, b):
    return jnp.dot(a, b, preferred_element_type=F32)


def dot_t(a, b):
    return lax.dot_general(a, b, (((1,), (1,)), ((), ())), preferred_element_type=F32)


def split_two(value):
    high = lax.reduce_precision(value, 8, 7)
    return high.astype(BF), (value - high).astype(BF)


def flipped(value, bits):
    result, weight = value * 0, 1
    while weight <= bits:
        digit = lax.rem(lax.div(value, weight), 2)
        result = result + weight * ((1 - digit) if bits & weight else digit)
        weight *= 2
    return result + weight * lax.div(value, weight)


def line_edges(planes):
    edges = []
    for k in range(planes):
        b = 1
        while b < planes and (k == 0 or b < (k & -k)):
            edges.append((k, b))
            b *= 2
    return edges


def remote(source, target, send_sem, recv_sem, other):
    return pltpu.make_async_remote_copy(
        src_ref=source,
        dst_ref=target,
        send_sem=send_sem,
        recv_sem=recv_sem,
        device_id={"ep": other},
        device_id_type=pl.DeviceIdType.MESH,
    )


def greet(partners):
    barrier = pltpu.get_barrier_semaphore()
    for other in partners:
        pl.semaphore_signal(
            barrier, inc=1, device_id={"ep": other}, device_id_type=pl.DeviceIdType.MESH
        )
    pl.semaphore_wait(barrier, len(partners))


def slot_numbers(shape, axis, cap, planes):
    number = lax.broadcasted_iota(jnp.int32, shape, axis).astype(F32)
    block = jnp.floor((number + 0.5) * (1.0 / cap))
    expert = jnp.floor((block + 0.5) * (1.0 / planes))
    return expert, block - expert * planes, number - block * cap


def fused_kernel(
    planes, cap, ring, lag,
    tokens_ref, cotangent_ref, aux_ref, gate_hbm, up_hbm, down_hbm,
    out_ref, gate_out,
    zbuf, pbuf, zaux, paux, choose_line, choose_plane, reorder, packed_line, packed_plane,
    xline, xplane, gate_acc, up_acc, down_acc, gate_w, up_w, down_w,
    rrecv, gsend, grecv, marks, mix_high, mix_low, zsend, zrecv, zgsend, zgrecv,
    load_sem, own_sem, aux_sem, zas_sem, zar_sem, pas_sem, par_sem, zs_sem, zr_sem, ps_sem, pr_sem,
    ls_sem, lr_sem, bs_sem, br_sem, keep_sem, rs_sem, rr_sem, gs_sem, gr_sem, hs_sem, hr_sem,
    hgs_sem, hgr_sem,
):
    me = lax.axis_index("ep")
    z, r = lax.div(me, PLANE), lax.rem(me, PLANE)
    supers, _, tok, cw = pbuf.shape
    steps = 4 * supers
    half = steps // 2
    owned, ff = gate_w.shape[1], gate_w.shape[3]
    group = planes * cap
    part = owned * group
    wide = PLANE * cap
    part_plane = owned * wide
    slots = PLANE * part
    deltas = ff // cw
    edges = line_edges(planes)

    def at(k, bits):
        return flipped(z, k) * PLANE + flipped(r, bits)

    core = lax.rem(r, 2)
    along_x, along_y, across, twin = (flipped(r, b) for b in (2, 4, 6, 1))
    near = along_x + core * (along_y - along_x)
    then = along_y + core * (along_x - along_y)

    def line_index(s, i):
        return 3 * s + (0, None, 1, 2)[i]

    own_aux = pltpu.make_async_copy(aux_ref, zaux.at[z], aux_sem.at[0])
    own_ranks = pltpu.make_async_copy(aux_ref.at[:, :LANES], paux.at[r], aux_sem.at[1])
    own_aux.start()
    own_ranks.start()
    for q in range(steps):
        source = tokens_ref if q < half else cotangent_ref
        columns = pl.ds((q % half) * cw, cw)
        s, i = q // 4, q % 4
        target = pbuf.at[s, r] if i == 1 else zbuf.at[line_index(s, i), z]
        pltpu.make_async_copy(source.at[:, columns], target, own_sem.at[q]).start()

    def first_loads(n, slot):
        depth = pl.ds(pl.multiple_of(n * cw, cw), cw)
        return [
            pltpu.make_async_copy(w.at[:, depth, :], buf.at[slot], load_sem.at[k, slot])
            for k, (w, buf) in enumerate(((gate_hbm, gate_w), (up_hbm, up_w)))
        ]

    def down_load(n, slot):
        depth = pl.ds(pl.multiple_of((n - half) * cw, cw), cw)
        return pltpu.make_async_copy(
            down_hbm.at[:, :, depth], down_w.at[slot], load_sem.at[2, slot]
        )

    for load in first_loads(0, 0):
        load.start()

    greet([at(k, 0) for k in range(1, planes)] + [at(0, b) for b in range(1, PLANE)])

    def line_hop(buf, sems, rems, index, e):
        k, b = edges[e]
        slot = flipped(z, k)
        return remote(
            buf.at[index + (slot,)], buf.at[index + (slot,)], sems.at[index + (e,)],
            rems.at[index + (slot,)], at(b, 0),
        )

    def line_arrived(buf, sems, rems, index, k):
        slot = flipped(z, k)
        remote(
            buf.at[index + (slot,)], buf.at[index + (slot,)], sems.at[index + (0,)],
            rems.at[index + (slot,)], at(1, 0),
        ).wait_recv()

    forwarded = sorted({k for k, b in edges if k}, reverse=True)
    plain = [k for k in range(1, planes) if k not in forwarded]
    data, ranks_of = (zbuf, zs_sem, zr_sem), (zaux, zas_sem, zar_sem)

    def line_start(kind, index):
        for e, (k, b) in enumerate(edges):
            if k == 0:
                line_hop(*kind, index, e).start()

    def line_forward(kind, index):
        for wanted in forwarded:
            line_arrived(*kind, index, wanted)
            for e, (k, b) in enumerate(edges):
                if k == wanted:
                    line_hop(*kind, index, e).start()

    def line_rest(kind, index):
        for k in plain:
            line_arrived(*kind, index, k)

    def line_own(s, i):
        a = line_index(s, i)
        pltpu.make_async_copy(zbuf.at[a, z], zbuf.at[a, z], own_sem.at[4 * s + i]).wait()
        line_start(data, (a,))

    hops = [
        [(r, near, 0), (r, then, 1), (r, twin, 2)],
        [(near, then, 3), (near, twin, 4), (then, twin, 5)],
        [(across, twin, 6)],
    ]

    def plane_hop(s, hop):
        slot, other, e = hop
        return remote(
            pbuf.at[s, slot], pbuf.at[s, slot], ps_sem.at[s, e], pr_sem.at[s, slot],
            z * PLANE + other,
        )

    def plane_arrived(s, slot):
        remote(
            pbuf.at[s, slot], pbuf.at[s, slot], ps_sem.at[s, 0], pr_sem.at[s, slot], at(0, 1)
        ).wait_recv()

    def plane_stage(s, stage):
        if stage == 0:
            pltpu.make_async_copy(pbuf.at[s, r], pbuf.at[s, r], own_sem.at[4 * s + 1]).wait()
        elif stage == 1:
            plane_arrived(s, near)
            plane_arrived(s, then)
        elif stage == 2:
            plane_arrived(s, across)
        else:
            for b in (1, 3, 5, 7):
                plane_arrived(s, flipped(r, b))
            return
        for hop in hops[stage]:
            plane_hop(s, hop).start()

    def ranks_hop(b):
        return remote(
            paux.at[r], paux.at[r], pas_sem.at[b], par_sem.at[r], at(0, b)
        )

    own_aux.wait()
    line_start(ranks_of, ())
    line_own(0, 0)
    own_ranks.wait()
    for b in range(1, PLANE):
        ranks_hop(b).start()
    plane_stage(0, 0)
    line_own(0, 2)

    token = lax.broadcasted_iota(jnp.int32, (part, planes * tok), 1).astype(F32)
    token_z = jnp.floor((token + 0.5) * (1.0 / tok))
    _, slot_z, place = slot_numbers((part, planes * tok), 0, cap, planes)
    same_z = token_z == slot_z
    lane = lax.broadcasted_iota(jnp.int32, (part, LANES), 1)
    expert = slot_numbers((part, LANES), 0, cap, planes)[0].astype(jnp.int32)
    line_forward(ranks_of, ())
    line_rest(ranks_of, ())
    line_forward(data, (0,))
    line_forward(data, (1,))
    ranks = zaux[:, :, :LANES].reshape(planes * tok, LANES)

    @pl.loop(0, PLANE)
    def _(p):
        first = (z * PLANE + p) * owned
        spread = jnp.where(lane == expert + first, 1.0, 0.0).astype(BF)
        rank_of = dot_t(spread, ranks)
        rows = pl.ds(pl.multiple_of(p * part, 16), part)
        choose_line[rows, :] = jnp.where(same_z & (rank_of == place), 1.0, 0.0).astype(BF)

    def choose_in_plane():
        for b in range(1, PLANE):
            other = flipped(r, b)
            remote(
                paux.at[other], paux.at[other], pas_sem.at[0], par_sem.at[other], at(0, 1)
            ).wait_recv()
        token = lax.broadcasted_iota(jnp.int32, (part_plane, PLANE * tok), 1).astype(F32)
        token_from = jnp.floor((token + 0.5) * (1.0 / tok))
        _, slot_from, place = slot_numbers((part_plane, PLANE * tok), 0, cap, PLANE)
        same = token_from == slot_from
        lane = lax.broadcasted_iota(jnp.int32, (part_plane, LANES), 1)
        expert = slot_numbers((part_plane, LANES), 0, cap, PLANE)[0].astype(jnp.int32)
        ranks = paux[...].reshape(PLANE * tok, LANES)

        @pl.loop(0, planes)
        def _(k):
            first = (k * PLANE + r) * owned
            spread = jnp.where(lane == expert + first, 1.0, 0.0).astype(BF)
            rank_of = dot_t(spread, ranks)
            rows = pl.ds(pl.multiple_of(k * part_plane, 16), part_plane)
            choose_plane[rows, :] = jnp.where(same & (rank_of == place), 1.0, 0.0).astype(BF)

        size = PLANE * group
        _, from_z, place = slot_numbers((size, size), 0, cap, planes)
        origin = slot_numbers((size, size), 0, cap, planes)[0]
        column = lax.broadcasted_iota(jnp.int32, (size, size), 1).astype(F32)
        wanted = (from_z * PLANE + origin) * cap + place
        reorder[...] = jnp.where(column == wanted, 1.0, 0.0).astype(BF)

    def line_give(a, b):
        other = flipped(r, b)
        slot = lax.rem(a, ring)
        return remote(
            packed_line.at[slot, other], xline.at[a, r], ls_sem.at[slot, other], lr_sem.at[a, r],
            at(0, b),
        )

    def line_keep(a):
        return pltpu.make_async_copy(
            packed_line.at[lax.rem(a, ring), r], xline.at[a, r], keep_sem.at[a]
        )

    def pack_line(a):
        line_rest(data, (a,))

        @pl.when(a >= ring)
        def _():
            for b in range(1, PLANE):
                line_give(a - ring, b).wait_send()

        picked = dot(choose_line[...], zbuf[a].reshape(planes * tok, cw)).astype(BF)
        packed_line[lax.rem(a, ring)] = picked.reshape(PLANE, part, cw)
        for b in (6, 7, 2, 4, 3, 5, 1):
            line_give(a, b).start()
        line_keep(a).start()

    def plane_give(s, k):
        other = flipped(z, k)
        return remote(
            packed_plane.at[s, other], xplane.at[s, z], bs_sem.at[s, k], br_sem.at[s, z], at(k, 0)
        )

    def plane_keep(s):
        return pltpu.make_async_copy(packed_plane.at[s, z], xplane.at[s, z], bs_sem.at[s, 0])

    def pack_plane(s):
        picked = dot(choose_plane[...], pbuf[s].reshape(PLANE * tok, cw)).astype(BF)
        packed_plane[s] = picked.reshape(planes, part_plane, cw)
        for k in range(planes - 1, 0, -1):
            plane_give(s, k).start()
        plane_keep(s).start()

    def rows_line(a):
        line_keep(a).wait()
        for b in range(1, PLANE):
            other = flipped(r, b)
            remote(
                xline.at[a, other], xline.at[a, other], ls_sem.at[0, 0], lr_sem.at[a, other],
                at(0, 1),
            ).wait_recv()
        return [
            xline[a, :, j * group:(j + 1) * group, :].reshape(PLANE * group, cw)
            for j in range(owned)
        ]

    def rows_plane(s):
        plane_keep(s).wait()
        for k in range(1, planes):
            other = flipped(z, k)
            remote(
                xplane.at[s, other], xplane.at[s, other], bs_sem.at[s, 0], br_sem.at[s, other],
                at(1, 0),
            ).wait_recv()
        return [
            dot(
                reorder[...],
                xplane[s, :, j * wide:(j + 1) * wide, :].reshape(PLANE * group, cw),
            ).astype(BF)
            for j in range(owned)
        ]

    def compute(s, i):
        n = 4 * s + i
        slot = i % 2
        rows = rows_plane(s) if i == 1 else rows_line(line_index(s, i))

        @pl.when(n + 1 < half)
        def _():
            for load in first_loads(n + 1, 1 - slot):
                load.start()

        @pl.when((n + 1 >= half) & (n + 1 < steps))
        def _():
            down_load(n + 1, 1 - slot).start()

        @pl.when(n + 1 == steps)
        def _():
            for load in first_loads(0, 1 - slot):
                load.start()

        @pl.when(n < half)
        def _():
            for load in first_loads(n, slot):
                load.wait()
            for j in range(owned):
                gate_acc[j] += dot(rows[j], gate_w[slot, j])
                up_acc[j] += dot(rows[j], up_w[slot, j])

        @pl.when(n >= half)
        def _():
            down_load(n, slot).wait()
            for j in range(owned):
                down_acc[j] += dot_t(rows[j], down_w[slot, j])

    def mix(p):
        _, slot_z, place = slot_numbers((tok, part), 1, cap, planes)
        first = (z * PLANE + p) * owned
        spread = jnp.where(lane == expert + first, 1.0, 0.0).astype(BF)
        columns = slice(p * part, (p + 1) * part)
        for k in range(planes):
            rows = slice(k * tok, (k + 1) * tok)
            values = zaux[k]
            rank_of = dot_t(values[:, :LANES], spread)
            hit = (rank_of == place) & (slot_z == float(k))
            marks[rows, columns] = jnp.where(hit, 1.0, 0.0).astype(BF)
            high = dot_t(values[:, LANES:2 * LANES], spread)
            low = dot_t(values[:, 2 * LANES:], spread)
            mix_high[rows, columns] = jnp.where(hit, high, 0.0).astype(BF)
            mix_low[rows, columns] = jnp.where(hit, low, 0.0).astype(BF)

    @pl.loop(0, supers + 2)
    def _(s):
        for i in range(4):
            @pl.when(s < supers)
            def _():
                if i == 1:
                    @pl.when(s == 0)
                    def _():
                        choose_in_plane()

                    plane_stage(s, 3)
                    pack_plane(s)
                else:
                    early = {0: ((0, 3), (1, 0)), 2: ((1, 2), (1, 3)), 3: ((2, 0),)}[i]
                    later = {0: (s + 1, 3), 2: (s + 2, 0), 3: (s + 2, 2)}[i]
                    follow = {0: (s, 3), 2: (s + 1, 0), 3: (s + 1, 2)}[i]

                    @pl.when(s == 0)
                    def _():
                        for item in early:
                            if item[0] < supers:
                                line_own(*item)

                    if i == 3:
                        @pl.when(s == 0)
                        def _():
                            if 2 < supers:
                                line_own(2, 2)

                    @pl.when((s >= 1) & (later[0] < supers))
                    def _():
                        line_own(*later)

                    pack_line(line_index(s, i))

                    @pl.when(follow[0] < supers)
                    def _():
                        line_forward(data, (line_index(*follow),))
                if i == 0:
                    @pl.when(s == 0)
                    def _():
                        for stage in (1, 2):
                            plane_stage(0, stage)
                        for other in range(1, supers):
                            plane_stage(other, 0)
                        for acc in (gate_acc, up_acc, down_acc):
                            acc[...] = jnp.zeros(acc.shape, F32)
                if i == 2:
                    @pl.when(s == 0)
                    def _():
                        for stage in (1, 2):
                            for other in range(1, supers):
                                plane_stage(other, stage)

            for p in range(PLANE):
                if p % 4 == i:
                    @pl.when(s == 1 + p // 4)
                    def _():
                        mix(p)

            back, at_step = (i - lag) // 4, (i - lag) % 4

            @pl.when((s + back >= 0) & (s + back < supers))
            def _():
                compute(s + back, at_step)

    column = lax.broadcasted_iota(jnp.int32, (group, LANES), 1)

    @pl.loop(0, PLANE)
    def _(p):
        rows = pl.ds(pl.multiple_of(p * group, 16), group)
        for j in range(owned):
            mine = slice(j * group, (j + 1) * group)
            gate_pre, up_pre, upward = gate_acc[j, rows, :], up_acc[j, rows, :], down_acc[j, rows, :]
            sigma = 1.0 / (1.0 + jnp.exp(-gate_pre))
            silu_val = gate_pre * sigma
            up_delta = upward * silu_val
            pick_gate = jnp.sum(up_delta * up_pre, axis=1, keepdims=True)
            gate_delta = upward * up_pre * sigma * (1.0 + gate_pre * (1.0 - sigma))
            for d in range(deltas):
                columns = slice(d * cw, (d + 1) * cw)
                xline[d, p, mine, :] = gate_delta[:, columns].astype(BF)
                xline[deltas + d, p, mine, :] = up_delta[:, columns].astype(BF)
            high = pick_gate.astype(BF).astype(F32)
            low = pick_gate - high
            both = jnp.where(column == 0, high, jnp.where(column == 1, low, 0.0))
            gsend[p, mine, :] = both.astype(BF)

    @pl.loop(supers * 3 - ring, supers * 3)
    def _(a):
        for b in range(1, PLANE):
            line_give(a, b).wait_send()

    returns = half

    def give(c, b):
        return remote(
            packed_line.at[c, flipped(r, b)], rrecv.at[c, r], rs_sem.at[c, b], rr_sem.at[c, r],
            at(0, b),
        )

    def keep(c):
        return pltpu.make_async_copy(packed_line.at[c, r], rrecv.at[c, r], rs_sem.at[c, 0])

    def give_gate(b):
        return remote(
            gsend.at[flipped(r, b)], grecv.at[r], gs_sem.at[b], gr_sem.at[r], at(0, b)
        )

    keep_gate = pltpu.make_async_copy(gsend.at[r], grecv.at[r], gs_sem.at[0])

    def home(c, k):
        slot = flipped(z, k)
        return remote(
            zsend.at[c, slot], zrecv.at[c, z], hs_sem.at[c, k], hr_sem.at[c, z], at(k, 0)
        )

    def home_gate(k):
        slot = flipped(z, k)
        return remote(
            zgsend.at[slot], zgrecv.at[z], hgs_sem.at[k], hgr_sem.at[z], at(k, 0)
        )

    for b in range(1, PLANE):
        give_gate(b).start()
    keep_gate.start()

    @pl.loop(0, returns // 2)
    def _(pair):
        for slot in range(2):
            c = 2 * pair + slot

            @pl.when(c + 1 < returns)
            def _():
                for load in first_loads(c + 1, 1 - slot):
                    load.start()

            for load in first_loads(c, slot):
                load.wait()
            for j in range(owned):
                mine = slice(j * group, (j + 1) * group)
                total = None
                for d in range(2 * deltas):
                    weight = (gate_w if d < deltas else up_w)[slot, j]
                    columns = slice((d % deltas) * cw, (d % deltas + 1) * cw)
                    rows = xline[d, :, mine, :].reshape(PLANE * group, cw)
                    term = dot_t(rows, weight[:, columns])
                    total = term if total is None else total + term
                packed_line[c, :, mine, :] = total.astype(BF).reshape(PLANE, group, cw)
            for b in (6, 7, 2, 4, 3, 5, 1):
                give(c, b).start()
            keep(c).start()

    own = pl.ds(pl.multiple_of(z * tok, tok), tok)

    @pl.loop(0, returns)
    def _(c):
        keep(c).wait()
        for b in range(1, PLANE):
            other = flipped(r, b)
            remote(
                rrecv.at[c, other], rrecv.at[c, other], rs_sem.at[c, 0], rr_sem.at[c, other],
                at(0, 1),
            ).wait_recv()
        rows = rrecv[c].reshape(slots, cw)
        total = dot(mix_high[...], rows) + dot(mix_low[...], rows)
        zsend[c] = total.astype(BF).reshape(planes, tok, cw)
        for k in range(planes - 1, 0, -1):
            home(c, k).start()
        columns = pl.ds(pl.multiple_of(c * cw, cw), cw)
        out_ref[:, columns] = dot(mix_high[own, :], rows) + dot(mix_low[own, :], rows)

        @pl.when(c == 1)
        def _():
            keep_gate.wait()
            for b in range(1, PLANE):
                other = flipped(r, b)
                remote(
                    grecv.at[other], grecv.at[other], gs_sem.at[0], gr_sem.at[other], at(0, 1)
                ).wait_recv()
            picked = grecv[...].reshape(slots, LANES).astype(F32)
            lane_of = lax.broadcasted_iota(jnp.int32, (slots, LANES), 1)
            number = slot_numbers((slots, LANES), 0, cap, planes)[0].astype(jnp.int32)
            here = lane_of == number + z * PLANE * owned
            high = jnp.sum(jnp.where(lane_of == 0, picked, 0.0), axis=1, keepdims=True)
            low = jnp.sum(jnp.where(lane_of == 1, picked, 0.0), axis=1, keepdims=True)
            high = jnp.where(here, high, 0.0).astype(BF)
            low = jnp.where(here, low, 0.0).astype(BF)
            gates = dot(marks[...], high) + dot(marks[...], low)
            zgsend[...] = gates.reshape(planes, tok, LANES)
            for k in range(1, planes):
                home_gate(k).start()

    @pl.loop(0, returns)
    def _(c):
        columns = pl.ds(pl.multiple_of(c * cw, cw), cw)
        total = out_ref[:, columns]
        for k in range(1, planes):
            slot = flipped(z, k)
            remote(
                zrecv.at[c, slot], zrecv.at[c, slot], hs_sem.at[c, 0], hr_sem.at[c, slot],
                at(1, 0),
            ).wait_recv()
            total = total + zrecv[c, slot].astype(F32)
        out_ref[:, columns] = total

    total = zgsend[z]
    for k in range(1, planes):
        slot = flipped(z, k)
        remote(
            zgrecv.at[slot], zgrecv.at[slot], hgs_sem.at[0], hgr_sem.at[slot], at(1, 0)
        ).wait_recv()
        total = total + zgrecv[slot]
    gate_out[...] = total

    for e in range(len(edges)):
        line_hop(*ranks_of, (), e).wait_send()
    for b in range(1, PLANE):
        ranks_hop(b).wait_send()
        give_gate(b).wait_send()
    for k in range(1, planes):
        home_gate(k).wait_send()

    @pl.loop(0, 3 * supers)
    def _(a):
        for e in range(len(edges)):
            line_hop(*data, (a,), e).wait_send()

    @pl.loop(0, supers)
    def _(s):
        for stage in hops:
            for hop in stage:
                plane_hop(s, hop).wait_send()
        for k in range(1, planes):
            plane_give(s, k).wait_send()

    @pl.loop(0, returns)
    def _(c):
        for b in range(1, PLANE):
            give(c, b).wait_send()
        for k in range(1, planes):
            home(c, k).wait_send()


def fused(planes, cap, tokens, cotangent, aux, gate_weight, up_weight, down_weight):
    tok, width = tokens.shape
    owned, _, ff = gate_weight.shape
    cw = COLUMNS
    half = width // cw
    supers = 2 * half // 4
    line = 3 * supers
    ring = half
    group = planes * cap
    part, rows = owned * group, PLANE * group
    part_plane = owned * PLANE * cap
    slots = PLANE * part
    edges = len(line_edges(planes))
    vmem = pl.BlockSpec(memory_space=pltpu.VMEM)
    hbm = pl.BlockSpec(memory_space=pl.ANY)
    dma = pltpu.SemaphoreType.DMA
    return pl.pallas_call(
        functools.partial(fused_kernel, planes, cap, ring, 5),
        out_shape=(
            jax.ShapeDtypeStruct((tok, width), F32),
            jax.ShapeDtypeStruct((tok, LANES), F32),
        ),
        in_specs=[hbm, hbm, vmem, hbm, hbm, hbm],
        out_specs=(vmem, vmem),
        scratch_shapes=[
            pltpu.VMEM((line, planes, tok, cw), BF),
            pltpu.VMEM((supers, PLANE, tok, cw), BF),
            pltpu.VMEM((planes,) + aux.shape, BF),
            pltpu.VMEM((PLANE, tok, LANES), BF),
            pltpu.VMEM((PLANE * part, planes * tok), BF),
            pltpu.VMEM((planes * part_plane, PLANE * tok), BF),
            pltpu.VMEM((rows, rows), BF),
            pltpu.VMEM((ring, PLANE, part, cw), BF),
            pltpu.VMEM((supers, planes, part_plane, cw), BF),
            pltpu.VMEM((line, PLANE, part, cw), BF),
            pltpu.VMEM((supers, planes, part_plane, cw), BF),
            pltpu.VMEM((owned, rows, ff), F32),
            pltpu.VMEM((owned, rows, ff), F32),
            pltpu.VMEM((owned, rows, ff), F32),
            pltpu.VMEM((2, owned, cw, ff), BF),
            pltpu.VMEM((2, owned, cw, ff), BF),
            pltpu.VMEM((2, owned, ff, cw), BF),
            pltpu.VMEM((half, PLANE, part, cw), BF),
            pltpu.VMEM((PLANE, part, LANES), BF),
            pltpu.VMEM((PLANE, part, LANES), BF),
            pltpu.VMEM((planes * tok, slots), BF),
            pltpu.VMEM((planes * tok, slots), BF),
            pltpu.VMEM((planes * tok, slots), BF),
            pltpu.VMEM((half, planes, tok, cw), BF),
            pltpu.VMEM((half, planes, tok, cw), BF),
            pltpu.VMEM((planes, tok, LANES), F32),
            pltpu.VMEM((planes, tok, LANES), F32),
            dma((3, 2)),
            dma((4 * supers,)),
            dma((2,)),
            dma((edges,)),
            dma((planes,)),
            dma((PLANE,)),
            dma((PLANE,)),
            dma((line, edges)),
            dma((line, planes)),
            dma((supers, 7)),
            dma((supers, PLANE)),
            dma((ring, PLANE)),
            dma((line, PLANE)),
            dma((supers, planes)),
            dma((supers, planes)),
            dma((line,)),
            dma((half, PLANE)),
            dma((half, PLANE)),
            dma((PLANE,)),
            dma((PLANE,)),
            dma((half, planes)),
            dma((half, planes)),
            dma((planes,)),
            dma((planes,)),
        ],
        compiler_params=pltpu.CompilerParams(
            collective_id=0, has_side_effects=True, vmem_limit_bytes=63 * 2**20
        ),
    )(tokens, cotangent, aux, gate_weight, up_weight, down_weight)


def by_planes(planes, tokens, cotangent, routing, expert_ids, gate_weight, up_weight, down_weight):
    owned = gate_weight.shape[0]
    experts = owned * planes * PLANE
    tok, top = expert_ids.shape
    cap = 5 * tok * top // (4 * experts)
    onehot = expert_ids[:, :, None] == jnp.arange(LANES, dtype=jnp.int32)[None, None, :]
    picked = jnp.any(onehot, axis=1)
    row = jnp.arange(tok, dtype=jnp.int32)
    lower = (row[:, None] > row[None, :]).astype(BF)
    rank = jnp.where(picked, dot(lower, picked.astype(BF)), -1.0).astype(BF)
    amount = jnp.sum(jnp.where(onehot, routing[:, :, None], 0.0), axis=1)
    amount_high, amount_low = split_two(amount)
    aux = jnp.concatenate([rank, amount_high, amount_low], axis=1)
    input_grad, gate_sum = fused(
        planes, cap, tokens, cotangent, aux, gate_weight, up_weight, down_weight
    )
    gate_grad = jnp.sum(jnp.where(onehot, gate_sum[:, None, :], 0.0), axis=2)
    return input_grad, gate_grad


def local(tokens, cotangent, routing, expert_ids, gate_weight, up_weight, down_weight):
    count = lax.axis_size("ep")
    owned = gate_weight.shape[0]
    experts = owned * count
    tok_rows, top = expert_ids.shape
    width = tokens.shape[1]
    cap = 5 * tok_rows * top // (4 * experts)
    slots = experts * cap

    onehot = expert_ids[:, :, None] == jnp.arange(experts, dtype=jnp.int32)[None, None, :]
    picked = jnp.any(onehot, axis=1)
    row = jnp.arange(tok_rows, dtype=jnp.int32)
    lower = (row[:, None] > row[None, :]).astype(BF)
    before = dot(lower, picked.astype(BF))
    rank = jnp.where(picked, before, -1.0).astype(BF)
    slot = jnp.arange(slots, dtype=jnp.int32)
    spread = (slot[:, None] // cap == jnp.arange(experts, dtype=jnp.int32)[None, :]).astype(BF)
    place = (slot % cap).astype(F32)
    rank_of = lax.dot_general(spread, rank, (((1,), (1,)), ((), ())), preferred_element_type=F32)
    choose = (rank_of == place[:, None]).astype(BF)
    rank_back = lax.dot_general(rank, spread, (((1,), (1,)), ((), ())), preferred_element_type=F32)
    choose_back = rank_back == place[None, :]

    def exchange(value):
        return lax.all_to_all(value, "ep", split_axis=0, concat_axis=0, tiled=True)

    def by_expert(value):
        value = value.reshape(count, owned, cap, value.shape[1])
        return value.transpose(1, 0, 2, 3).reshape(owned, count * cap, value.shape[3])

    def by_source(value):
        value = value.reshape(owned, count, cap, value.shape[2])
        return value.transpose(1, 0, 2, 3).reshape(slots, value.shape[3])

    inputs = by_expert(exchange(dot(choose, tokens).astype(BF)))
    grads_in = by_expert(exchange(dot(choose, cotangent).astype(BF)))
    gate_pre = jnp.einsum("erd,edf->erf", inputs, gate_weight, preferred_element_type=F32)
    up_pre = jnp.einsum("erd,edf->erf", inputs, up_weight, preferred_element_type=F32)
    upward = jnp.einsum("erd,efd->erf", grads_in, down_weight, preferred_element_type=F32)
    sigma = jax.nn.sigmoid(gate_pre)
    silu_val = gate_pre * sigma
    pick_gate = jnp.sum(silu_val * up_pre * upward, axis=2, keepdims=True)
    gate_delta = (upward * up_pre * sigma * (1.0 + gate_pre * (1.0 - sigma))).astype(BF)
    up_delta = (upward * silu_val).astype(BF)
    deltas = jnp.concatenate([gate_delta, up_delta], axis=2)
    joined = jnp.concatenate([gate_weight, up_weight], axis=2)

    half = width // 2
    gate_high, gate_low = split_two(pick_gate)
    lane = jnp.arange(128, dtype=jnp.int32)[None, None, :]
    gate_cols = jnp.where(lane == 0, gate_high, jnp.where(lane == 1, gate_low, jnp.zeros((), BF)))
    first = jnp.einsum("erf,edf->erd", deltas, joined[:, :half], preferred_element_type=F32).astype(BF)
    second = jnp.einsum("erf,edf->erd", deltas, joined[:, half:], preferred_element_type=F32).astype(BF)
    back_a = exchange(by_source(jnp.concatenate([first, gate_cols], axis=2)))
    back_b = exchange(by_source(second))

    amount = jnp.sum(jnp.where(onehot, routing[:, :, None], 0.0), axis=1)
    amount_high, amount_low = split_two(amount)
    zero = jnp.zeros((), BF)

    def mix(part):
        wide = lax.dot_general(part, spread, (((1,), (1,)), ((), ())), preferred_element_type=F32)
        return jnp.where(choose_back, wide.astype(BF), zero)

    mixing = jnp.concatenate([mix(amount_high), mix(amount_low)], axis=0)

    def combine(value):
        both = dot(mixing, value)
        return both[:tok_rows] + both[tok_rows:]

    weighted = jnp.concatenate([combine(back_a[:, :half]), combine(back_b)], axis=1)
    gates = back_a[:, half:half + 2].T

    def gate_part(i):
        return dot(jnp.where(choose_back, gates[i][None, :], zero), spread)

    gate_sum = gate_part(0) + gate_part(1)
    gate_grad = jnp.sum(jnp.where(onehot, gate_sum[:, None, :], 0.0), axis=2)
    input_grad = lax.psum_scatter(weighted, "hid", scatter_dimension=1, tiled=True)
    return (input_grad, lax.psum(gate_grad, "hid"))


def solution(mesh):
    placed = (
        P(("rep", "ep"), None),
        P(("rep", "ep"), None),
        P(("rep", "ep"), None),
        P(("rep", "ep"), None),
        P("ep", None, "hid"),
        P("ep", None, "hid"),
        P("ep", "hid", None),
    )
    count = mesh.shape["ep"]
    planes = count // PLANE
    direct = (
        mesh.shape["rep"] * mesh.shape["hid"] == 1
        and count % PLANE == 0
        and planes > 1
        and planes & (planes - 1) == 0
    )

    def run(tokens, cotangent, routing, expert_ids, gate_weight, *rest):
        tok, top = expert_ids.shape
        owned, width, ff = gate_weight.shape
        cap = 5 * tok * top // (4 * owned * count)
        fits = (
            direct
            and owned * count <= LANES
            and planes * cap % 16 == 0
            and tok % 16 == 0
            and width % (4 * COLUMNS) == 0
            and ff % COLUMNS == 0
            and 2 * ff // COLUMNS <= 6 * width // (4 * COLUMNS)
        )
        body = functools.partial(by_planes, planes) if fits else local
        return body(tokens, cotangent, routing, expert_ids, gate_weight, *rest)

    return jax.shard_map(
        run,
        mesh=mesh,
        in_specs=placed,
        out_specs=(P(("rep", "ep"), "hid"), P(("rep", "ep"), None)),
        check_vma=False,
    )
```

profile of v0, /device:TPU:0, one launch (start us, length us, event | category | flops | bytes accessed | tf_op | source)
XLA Modules:
  0.0 213.6 jit_solution(87832356909692370)
XLA Ops:
  0.6 0.8 copy.12
  1.4 0.8 copy.14
  2.2 0.3 select_reduce_fusion.1
  2.6 0.3 fusion.1
  2.8 0.1 fusion
  3.0 0.7 pad_maximum_fusion.aux_ref
  3.6 205.7 %shard_map.86 = (f32[128,2048]{1,0:T(8,128)}, f32[128,128]{1,0:T(8,128)}) custom-call(bf16[128,2048]{1,0:T(8,128)(2,1)} %tokens_ref.1, bf16[128,2048]{1,0:T(8,128)(2,1)} %cotangent_ref.1, bf16[128,384]{1,0:T(8,128)(2,1)} %pad_maximum_fusion.aux_ref, bf16[2,2048,768]{2,1,0:T(8,128)(2,1)} %gate_hbm.1, bf16[2,2048,768]{2,1,0:T(8,128)(2,1)} %up_hbm.1, ...), custom_call_target="tpu_custom_call" | custom-call | tf_op jit(solution)/shard_map/pallas_call | solution.py:658
  209.4 1.2 select_reduce_fusion
  210.6 0.7 copy.15
  211.3 2.3 %copy.18 = f32[128,2048]{1,0:T(8,128)} copy(f32[128,2048]{1,0:T(8,128)} %get-tuple-element.12) | data formatting | bytes 2097152
  (1 shorter events, 0.0 us)
where the time goes:
time: 215 us; the launch traced here: 214 us
  Pallas kernels  206 us (96%)
  local copies, waits for them, and re-layouts  4.53 us (2%)
  other arithmetic  2.48 us (1%)
    pallas_call x1, Pallas kernels, fused(): pl.pallas_call(functools.partial(fused_kernel, planes, cap, ring, 5), out...  206 us
    unnamed x4, local copies, waits for them, and re-layouts  4.53 us

commit v1 on v0

--- a/solution.py
+++ b/solution.py
@@ -57,12 +57,14 @@
     )
 
 
-def greet(partners):
+def greet(partners, meanwhile=None):
     barrier = pltpu.get_barrier_semaphore()
     for other in partners:
         pl.semaphore_signal(
             barrier, inc=1, device_id={"ep": other}, device_id_type=pl.DeviceIdType.MESH
         )
+    if meanwhile is not None:
+        meanwhile()
     pl.semaphore_wait(barrier, len(partners))
 
 
@@ -75,12 +77,12 @@
 
 def fused_kernel(
     planes, cap, ring, lag,
-    tokens_ref, cotangent_ref, aux_ref, gate_hbm, up_hbm, down_hbm,
+    tokens_ref, cotangent_ref, weights_ref, ids_ref, gate_hbm, up_hbm, down_hbm,
     out_ref, gate_out,
-    zbuf, pbuf, zaux, paux, choose_line, choose_plane, reorder, packed_line, packed_plane,
+    zbuf, pbuf, zrank, zamount, paux, choose_line, choose_plane, reorder, packed_line, packed_plane,
     xline, xplane, gate_acc, up_acc, down_acc, gate_w, up_w, down_w,
     rrecv, gsend, grecv, marks, mix_high, mix_low, zsend, zrecv, zgsend, zgrecv,
-    load_sem, own_sem, aux_sem, zas_sem, zar_sem, pas_sem, par_sem, zs_sem, zr_sem, ps_sem, pr_sem,
+    load_sem, own_sem, zks_sem, zkr_sem, zas_sem, zar_sem, pas_sem, par_sem, zs_sem, zr_sem, ps_sem, pr_sem,
     ls_sem, lr_sem, bs_sem, br_sem, keep_sem, rs_sem, rr_sem, gs_sem, gr_sem, hs_sem, hr_sem,
     hgs_sem, hgr_sem,
 ):
@@ -107,17 +109,13 @@
     then = along_y + core * (along_x - along_y)
 
     def line_index(s, i):
-        return 3 * s + (0, None, 1, 2)[i]
-
-    own_aux = pltpu.make_async_copy(aux_ref, zaux.at[z], aux_sem.at[0])
-    own_ranks = pltpu.make_async_copy(aux_ref.at[:, :LANES], paux.at[r], aux_sem.at[1])
-    own_aux.start()
-    own_ranks.start()
+        return 3 * s + (0, 1, None, 2)[i]
+
     for q in range(steps):
         source = tokens_ref if q < half else cotangent_ref
         columns = pl.ds((q % half) * cw, cw)
         s, i = q // 4, q % 4
-        target = pbuf.at[s, r] if i == 1 else zbuf.at[line_index(s, i), z]
+        target = pbuf.at[s, r] if i == 2 else zbuf.at[line_index(s, i), z]
         pltpu.make_async_copy(source.at[:, columns], target, own_sem.at[q]).start()
 
     def first_loads(n, slot):
@@ -136,7 +134,36 @@
     for load in first_loads(0, 0):
         load.start()
 
-    greet([at(k, 0) for k in range(1, planes)] + [at(0, b) for b in range(1, PLANE)])
+    top = ids_ref.shape[0]
+    expert_row = lax.broadcasted_iota(jnp.int32, (LANES, tok), 0)
+    named = jnp.zeros((LANES, tok), F32)
+    amount = jnp.zeros((LANES, tok), F32)
+    for k in range(top):
+        hit = expert_row == ids_ref[k:k + 1, :]
+        named = jnp.where(hit, 1.0, named)
+        amount = jnp.where(hit, weights_ref[k:k + 1, :], amount)
+    earlier = lax.broadcasted_iota(jnp.int32, (tok, tok), 0)
+    earlier = earlier < lax.broadcasted_iota(jnp.int32, (tok, tok), 1)
+    rank = dot(named.astype(BF), jnp.where(earlier, 1.0, 0.0).astype(BF))
+    rank = jnp.where(named > 0.0, rank, -1.0).T.astype(BF)
+    zrank[z] = rank
+    paux[r] = rank
+    amount = amount.T
+    amount_high = amount.astype(BF)
+    zamount[z, :, :LANES] = amount_high
+    zamount[z, :, LANES:] = (amount - amount_high.astype(F32)).astype(BF)
+
+    def prepare():
+        for acc in (gate_acc, up_acc, down_acc):
+            acc[...] = jnp.zeros(acc.shape, F32)
+        size = PLANE * group
+        _, from_z, place = slot_numbers((size, size), 0, cap, planes)
+        origin = slot_numbers((size, size), 0, cap, planes)[0]
+        column = lax.broadcasted_iota(jnp.int32, (size, size), 1).astype(F32)
+        wanted = (from_z * PLANE + origin) * cap + place
+        reorder[...] = jnp.where(column == wanted, 1.0, 0.0).astype(BF)
+
+    greet([at(k, 0) for k in range(1, planes)] + [at(0, b) for b in range(1, PLANE)], prepare)
 
     def line_hop(buf, sems, rems, index, e):
         k, b = edges[e]
@@ -155,7 +182,7 @@
 
     forwarded = sorted({k for k, b in edges if k}, reverse=True)
     plain = [k for k in range(1, planes) if k not in forwarded]
-    data, ranks_of = (zbuf, zs_sem, zr_sem), (zaux, zas_sem, zar_sem)
+    data = (zbuf, zs_sem, zr_sem)
 
     def line_start(kind, index):
         for e, (k, b) in enumerate(edges):
@@ -173,6 +200,23 @@
         for k in plain:
             line_arrived(*kind, index, k)
 
+    def straight(buf, sems, rems, k):
+        return remote(buf.at[z], buf.at[z], sems.at[k], rems.at[z], at(k, 0))
+
+    def straight_arrived(buf, sems, rems):
+        for k in range(1, planes):
+            slot = flipped(z, k)
+            remote(
+                buf.at[slot], buf.at[slot], sems.at[0], rems.at[slot], at(1, 0)
+            ).wait_recv()
+
+    def first_straight(k):
+        return remote(
+            zbuf.at[0, z], zbuf.at[0, z], zs_sem.at[0, k - 1], zr_sem.at[0, z], at(k, 0)
+        )
+
+    line_ranks, line_amounts = (zrank, zks_sem, zkr_sem), (zamount, zas_sem, zar_sem)
+
     def line_own(s, i):
         a = line_index(s, i)
         pltpu.make_async_copy(zbuf.at[a, z], zbuf.at[a, z], own_sem.at[4 * s + i]).wait()
@@ -198,7 +242,7 @@
 
     def plane_stage(s, stage):
         if stage == 0:
-            pltpu.make_async_copy(pbuf.at[s, r], pbuf.at[s, r], own_sem.at[4 * s + 1]).wait()
+            pltpu.make_async_copy(pbuf.at[s, r], pbuf.at[s, r], own_sem.at[4 * s + 2]).wait()
         elif stage == 1:
             plane_arrived(s, near)
             plane_arrived(s, then)
@@ -216,14 +260,17 @@
             paux.at[r], paux.at[r], pas_sem.at[b], par_sem.at[r], at(0, b)
         )
 
-    own_aux.wait()
-    line_start(ranks_of, ())
-    line_own(0, 0)
-    own_ranks.wait()
+    for k in range(1, planes):
+        straight(*line_ranks, k).start()
+    pltpu.make_async_copy(zbuf.at[0, z], zbuf.at[0, z], own_sem.at[0]).wait()
+    for k in range(1, planes):
+        first_straight(k).start()
     for b in range(1, PLANE):
         ranks_hop(b).start()
     plane_stage(0, 0)
-    line_own(0, 2)
+    line_own(0, 1)
+    for s in range(1, supers):
+        plane_stage(s, 0)
 
     token = lax.broadcasted_iota(jnp.int32, (part, planes * tok), 1).astype(F32)
     token_z = jnp.floor((token + 0.5) * (1.0 / tok))
@@ -231,11 +278,8 @@
     same_z = token_z == slot_z
     lane = lax.broadcasted_iota(jnp.int32, (part, LANES), 1)
     expert = slot_numbers((part, LANES), 0, cap, planes)[0].astype(jnp.int32)
-    line_forward(ranks_of, ())
-    line_rest(ranks_of, ())
-    line_forward(data, (0,))
-    line_forward(data, (1,))
-    ranks = zaux[:, :, :LANES].reshape(planes * tok, LANES)
+    straight_arrived(*line_ranks)
+    ranks = zrank[...].reshape(planes * tok, LANES)
 
     @pl.loop(0, PLANE)
     def _(p):
@@ -267,12 +311,6 @@
             rows = pl.ds(pl.multiple_of(k * part_plane, 16), part_plane)
             choose_plane[rows, :] = jnp.where(same & (rank_of == place), 1.0, 0.0).astype(BF)
 
-        size = PLANE * group
-        _, from_z, place = slot_numbers((size, size), 0, cap, planes)
-        origin = slot_numbers((size, size), 0, cap, planes)[0]
-        column = lax.broadcasted_iota(jnp.int32, (size, size), 1).astype(F32)
-        wanted = (from_z * PLANE + origin) * cap + place
-        reorder[...] = jnp.where(column == wanted, 1.0, 0.0).astype(BF)
 
     def line_give(a, b):
         other = flipped(r, b)
@@ -289,6 +327,11 @@
 
     def pack_line(a):
         line_rest(data, (a,))
+
+        @pl.when(a == 0)
+        def _():
+            for k in forwarded:
+                line_arrived(*data, (0,), k)
 
         @pl.when(a >= ring)
         def _():
@@ -349,7 +392,7 @@
     def compute(s, i):
         n = 4 * s + i
         slot = i % 2
-        rows = rows_plane(s) if i == 1 else rows_line(line_index(s, i))
+        rows = rows_plane(s) if i == 2 else rows_line(line_index(s, i))
 
         @pl.when(n + 1 < half)
         def _():
@@ -386,12 +429,12 @@
         columns = slice(p * part, (p + 1) * part)
         for k in range(planes):
             rows = slice(k * tok, (k + 1) * tok)
-            values = zaux[k]
-            rank_of = dot_t(values[:, :LANES], spread)
+            values = zamount[k]
+            rank_of = dot_t(zrank[k], spread)
             hit = (rank_of == place) & (slot_z == float(k))
             marks[rows, columns] = jnp.where(hit, 1.0, 0.0).astype(BF)
-            high = dot_t(values[:, LANES:2 * LANES], spread)
-            low = dot_t(values[:, 2 * LANES:], spread)
+            high = dot_t(values[:, :LANES], spread)
+            low = dot_t(values[:, LANES:], spread)
             mix_high[rows, columns] = jnp.where(hit, high, 0.0).astype(BF)
             mix_low[rows, columns] = jnp.where(hit, low, 0.0).astype(BF)
 
@@ -400,7 +443,7 @@
         for i in range(4):
             @pl.when(s < supers)
             def _():
-                if i == 1:
+                if i == 2:
                     @pl.when(s == 0)
                     def _():
                         choose_in_plane()
@@ -408,9 +451,9 @@
                     plane_stage(s, 3)
                     pack_plane(s)
                 else:
-                    early = {0: ((0, 3), (1, 0)), 2: ((1, 2), (1, 3)), 3: ((2, 0),)}[i]
-                    later = {0: (s + 1, 3), 2: (s + 2, 0), 3: (s + 2, 2)}[i]
-                    follow = {0: (s, 3), 2: (s + 1, 0), 3: (s + 1, 2)}[i]
+                    early = {0: ((0, 3), (1, 0)), 1: ((1, 1), (1, 3)), 3: ((2, 0), (2, 1))}[i]
+                    later = {0: (s + 1, 3), 1: (s + 2, 0), 3: (s + 2, 1)}[i]
+                    follow = {0: (s, 3), 1: (s + 1, 0), 3: (s + 1, 1)}[i]
 
                     @pl.when(s == 0)
                     def _():
@@ -418,17 +461,18 @@
                             if item[0] < supers:
                                 line_own(*item)
 
-                    if i == 3:
-                        @pl.when(s == 0)
-                        def _():
-                            if 2 < supers:
-                                line_own(2, 2)
-
                     @pl.when((s >= 1) & (later[0] < supers))
                     def _():
                         line_own(*later)
 
                     pack_line(line_index(s, i))
+
+                    if i == 0:
+                        @pl.when(s == 0)
+                        def _():
+                            for k in range(1, planes):
+                                straight(*line_amounts, k).start()
+                            line_forward(data, (1,))
 
                     @pl.when(follow[0] < supers)
                     def _():
@@ -438,10 +482,6 @@
                     def _():
                         for stage in (1, 2):
                             plane_stage(0, stage)
-                        for other in range(1, supers):
-                            plane_stage(other, 0)
-                        for acc in (gate_acc, up_acc, down_acc):
-                            acc[...] = jnp.zeros(acc.shape, F32)
                 if i == 2:
                     @pl.when(s == 0)
                     def _():
@@ -453,6 +493,8 @@
                 if p % 4 == i:
                     @pl.when(s == 1 + p // 4)
                     def _():
+                        if p == 0:
+                            straight_arrived(*line_amounts)
                         mix(p)
 
             back, at_step = (i - lag) // 4, (i - lag) % 4
@@ -608,17 +650,22 @@
             zgrecv.at[slot], zgrecv.at[slot], hgs_sem.at[0], hgr_sem.at[slot], at(1, 0)
         ).wait_recv()
         total = total + zgrecv[slot]
-    gate_out[...] = total
-
-    for e in range(len(edges)):
-        line_hop(*ranks_of, (), e).wait_send()
+    total = total.T
+    for k in range(top):
+        hit = expert_row == ids_ref[k:k + 1, :]
+        gate_out[k:k + 1, :] = jnp.sum(jnp.where(hit, total, 0.0), axis=0, keepdims=True)
+
+    for k in range(1, planes):
+        straight(*line_ranks, k).wait_send()
+        straight(*line_amounts, k).wait_send()
+        first_straight(k).wait_send()
     for b in range(1, PLANE):
         ranks_hop(b).wait_send()
         give_gate(b).wait_send()
     for k in range(1, planes):
         home_gate(k).wait_send()
 
-    @pl.loop(0, 3 * supers)
+    @pl.loop(1, 3 * supers)
     def _(a):
         for e in range(len(edges)):
             line_hop(*data, (a,), e).wait_send()
@@ -639,7 +686,7 @@
             home(c, k).wait_send()
 
 
-def fused(planes, cap, tokens, cotangent, aux, gate_weight, up_weight, down_weight):
+def fused(planes, cap, tokens, cotangent, weights, ids, gate_weight, up_weight, down_weight):
     tok, width = tokens.shape
     owned, _, ff = gate_weight.shape
     cw = COLUMNS
@@ -659,14 +706,15 @@
         functools.partial(fused_kernel, planes, cap, ring, 5),
         out_shape=(
             jax.ShapeDtypeStruct((tok, width), F32),
-            jax.ShapeDtypeStruct((tok, LANES), F32),
+            jax.ShapeDtypeStruct(ids.shape, F32),
         ),
-        in_specs=[hbm, hbm, vmem, hbm, hbm, hbm],
+        in_specs=[hbm, hbm, vmem, vmem, hbm, hbm, hbm],
         out_specs=(vmem, vmem),
         scratch_shapes=[
             pltpu.VMEM((line, planes, tok, cw), BF),
             pltpu.VMEM((supers, PLANE, tok, cw), BF),
-            pltpu.VMEM((planes,) + aux.shape, BF),
+            pltpu.VMEM((planes, tok, LANES), BF),
+            pltpu.VMEM((planes, tok, 2 * LANES), BF),
             pltpu.VMEM((PLANE, tok, LANES), BF),
             pltpu.VMEM((PLANE * part, planes * tok), BF),
             pltpu.VMEM((planes * part_plane, PLANE * tok), BF),
@@ -693,8 +741,9 @@
             pltpu.VMEM((planes, tok, LANES), F32),
             dma((3, 2)),
             dma((4 * supers,)),
-            dma((2,)),
-            dma((edges,)),
+            dma((planes,)),
+            dma((planes,)),
+            dma((planes,)),
             dma((planes,)),
             dma((PLANE,)),
             dma((PLANE,)),
@@ -719,7 +768,7 @@
         compiler_params=pltpu.CompilerParams(
             collective_id=0, has_side_effects=True, vmem_limit_bytes=63 * 2**20
         ),
-    )(tokens, cotangent, aux, gate_weight, up_weight, down_weight)
+    )(tokens, cotangent, weights, ids, gate_weight, up_weight, down_weight)
 
 
 def by_planes(planes, tokens, cotangent, routing, expert_ids, gate_weight, up_weight, down_weight):
@@ -727,19 +776,11 @@
     experts = owned * planes * PLANE
     tok, top = expert_ids.shape
     cap = 5 * tok * top // (4 * experts)
-    onehot = expert_ids[:, :, None] == jnp.arange(LANES, dtype=jnp.int32)[None, None, :]
-    picked = jnp.any(onehot, axis=1)
-    row = jnp.arange(tok, dtype=jnp.int32)
-    lower = (row[:, None] > row[None, :]).astype(BF)
-    rank = jnp.where(picked, dot(lower, picked.astype(BF)), -1.0).astype(BF)
-    amount = jnp.sum(jnp.where(onehot, routing[:, :, None], 0.0), axis=1)
-    amount_high, amount_low = split_two(amount)
-    aux = jnp.concatenate([rank, amount_high, amount_low], axis=1)
-    input_grad, gate_sum = fused(
-        planes, cap, tokens, cotangent, aux, gate_weight, up_weight, down_weight
+    input_grad, gate_grad = fused(
+        planes, cap, tokens, cotangent, routing.T, expert_ids.T, gate_weight, up_weight,
+        down_weight,
     )
-    gate_grad = jnp.sum(jnp.where(onehot, gate_sum[:, None, :], 0.0), axis=2)
-    return input_grad, gate_grad
+    return input_grad, gate_grad.T
 
 
 def local(tokens, cotangent, routing, expert_ids, gate_weight, up_weight, down_weight):
@@ -851,7 +892,7 @@
             direct
             and owned * count <= LANES
             and planes * cap % 16 == 0
-            and tok % 16 == 0
+            and tok % LANES == 0
             and width % (4 * COLUMNS) == 0
             and ff % COLUMNS == 0
             and 2 * ff // COLUMNS <= 6 * width // (4 * COLUMNS)

time: 215 us -> 201 us (0.935)
  Pallas kernels: 206 us -> 196 us
  other arithmetic: 2.48 us -> 0 us
    pallas_call x1, Pallas kernels: 206 us -> 196 us  [fused(): pl.pallas_call(functools.partial(fused_kernel, planes, cap, ring, 5), out...]
    unnamed x4 -> x2, local copies, waits for them, and re-layouts: 4.53 us -> 3.57 us
where the time goes in v1:
time: 201 us; the launch traced here: 200 us
  Pallas kernels  196 us (98%)
  local copies, waits for them, and re-layouts  3.57 us (2%)
    pallas_call x1, Pallas kernels, fused(): pl.pallas_call(functools.partial(fused_kernel, planes, cap, ring, 5), out...  196 us

profile of v1, /device:TPU:0, one launch (start us, length us, event | category | flops | bytes accessed | tf_op | source)
XLA Modules:
  0.0 200.4 jit_solution(6171044199137123246)
XLA Ops:
  0.6 196.2 %shard_map.86 = (f32[128,2048]{1,0:T(8,128)}, f32[8,128]{1,0:T(8,128)}) custom-call(bf16[128,2048]{1,0:T(8,128)(2,1)} %tokens_ref.1, bf16[128,2048]{1,0:T(8,128)(2,1)} %cotangent_ref.1, f32[8,128]{1,0:T(8,128)} %bitcast.3, s32[8,128]{1,0:T(8,128)} %bitcast.4, bf16[2,2048,768]{2,1,0:T(8,128)(2,1)} %gate_hbm.1, bf16[2,2048,768]{2,1,0:T(8,128)(2,1)} %up_hbm.1, ...), custom_call_target="tpu_custom_call" | custom-call | tf_op jit(solution)/shard_map/pallas_call | solution.py:705
  196.8 2.3 %copy.11 = f32[128,2048]{1,0:T(8,128)} copy(f32[128,2048]{1,0:T(8,128)} %get-tuple-element.8) | data formatting | bytes 2097152
  199.1 1.3 copy.12

commit v2 on v1

--- a/solution.py
+++ b/solution.py
@@ -12,6 +12,7 @@
 PLANE = 8
 LANES = 128
 COLUMNS = 256
+BEHIND, LAST = 2, 2
 
 
 def dot(a, b):
@@ -80,8 +81,8 @@
     tokens_ref, cotangent_ref, weights_ref, ids_ref, gate_hbm, up_hbm, down_hbm,
     out_ref, gate_out,
     zbuf, pbuf, zrank, zamount, paux, choose_line, choose_plane, reorder, packed_line, packed_plane,
-    xline, xplane, gate_acc, up_acc, down_acc, gate_w, up_w, down_w,
-    rrecv, gsend, grecv, marks, mix_high, mix_low, zsend, zrecv, zgsend, zgrecv,
+    xline, xplane, gate_acc, up_acc, down_acc, slope, gate_w, up_w, down_w,
+    rrecv, gsend, grecv, marks, mix_high, mix_low, zrecv, zgsend, zgrecv,
     load_sem, own_sem, zks_sem, zkr_sem, zas_sem, zar_sem, pas_sem, par_sem, zs_sem, zr_sem, ps_sem, pr_sem,
     ls_sem, lr_sem, bs_sem, br_sem, keep_sem, rs_sem, rr_sem, gs_sem, gr_sem, hs_sem, hr_sem,
     hgs_sem, hgr_sem,
@@ -340,7 +341,7 @@
 
         picked = dot(choose_line[...], zbuf[a].reshape(planes * tok, cw)).astype(BF)
         packed_line[lax.rem(a, ring)] = picked.reshape(PLANE, part, cw)
-        for b in (6, 7, 2, 4, 3, 5, 1):
+        for b in (2, 4, 6, 3, 5, 7, 1):
             line_give(a, b).start()
         line_keep(a).start()
 
@@ -356,7 +357,7 @@
     def pack_plane(s):
         picked = dot(choose_plane[...], pbuf[s].reshape(PLANE * tok, cw)).astype(BF)
         packed_plane[s] = picked.reshape(planes, part_plane, cw)
-        for k in range(planes - 1, 0, -1):
+        for k in range(1, planes):
             plane_give(s, k).start()
         plane_keep(s).start()
 
@@ -408,6 +409,11 @@
             for load in first_loads(0, 1 - slot):
                 load.start()
 
+        if i == half % 4:
+            @pl.when(n == half)
+            def _():
+                activate()
+
         @pl.when(n < half)
         def _():
             for load in first_loads(n, slot):
@@ -421,6 +427,16 @@
             down_load(n, slot).wait()
             for j in range(owned):
                 down_acc[j] += dot_t(rows[j], down_w[slot, j])
+
+    def activate():
+        @pl.loop(0, PLANE)
+        def _(p):
+            rows = pl.ds(pl.multiple_of(p * group, 16), group)
+            for j in range(owned):
+                gate_pre = gate_acc[j, rows, :]
+                sigma = 1.0 / (1.0 + jnp.exp(-gate_pre))
+                gate_acc[j, rows, :] = gate_pre * sigma
+                slope[j, rows, :] = sigma * (1.0 + gate_pre * (1.0 - sigma))
 
     def mix(p):
         _, slot_z, place = slot_numbers((tok, part), 1, cap, planes)
@@ -510,12 +526,10 @@
         rows = pl.ds(pl.multiple_of(p * group, 16), group)
         for j in range(owned):
             mine = slice(j * group, (j + 1) * group)
-            gate_pre, up_pre, upward = gate_acc[j, rows, :], up_acc[j, rows, :], down_acc[j, rows, :]
-            sigma = 1.0 / (1.0 + jnp.exp(-gate_pre))
-            silu_val = gate_pre * sigma
+            silu_val, up_pre, upward = gate_acc[j, rows, :], up_acc[j, rows, :], down_acc[j, rows, :]
             up_delta = upward * silu_val
             pick_gate = jnp.sum(up_delta * up_pre, axis=1, keepdims=True)
-            gate_delta = upward * up_pre * sigma * (1.0 + gate_pre * (1.0 - sigma))
+            gate_delta = upward * up_pre * slope[j, rows, :]
             for d in range(deltas):
                 columns = slice(d * cw, (d + 1) * cw)
                 xline[d, p, mine, :] = gate_delta[:, columns].astype(BF)
@@ -530,6 +544,14 @@
         for b in range(1, PLANE):
             line_give(a, b).wait_send()
 
+    for k in range(1, planes):
+        first_straight(k).wait_send()
+
+    @pl.loop(1, 3 * supers)
+    def _(a):
+        for e in range(len(edges)):
+            line_hop(*data, (a,), e).wait_send()
+
     returns = half
 
     def give(c, b):
@@ -551,7 +573,7 @@
     def home(c, k):
         slot = flipped(z, k)
         return remote(
-            zsend.at[c, slot], zrecv.at[c, z], hs_sem.at[c, k], hr_sem.at[c, z], at(k, 0)
+            zbuf.at[c, slot], zrecv.at[c, z], hs_sem.at[c, k], hr_sem.at[c, z], at(k, 0)
         )
 
     def home_gate(k):
@@ -564,36 +586,33 @@
         give_gate(b).start()
     keep_gate.start()
 
-    @pl.loop(0, returns // 2)
-    def _(pair):
-        for slot in range(2):
-            c = 2 * pair + slot
-
-            @pl.when(c + 1 < returns)
-            def _():
-                for load in first_loads(c + 1, 1 - slot):
-                    load.start()
-
-            for load in first_loads(c, slot):
-                load.wait()
-            for j in range(owned):
-                mine = slice(j * group, (j + 1) * group)
-                total = None
-                for d in range(2 * deltas):
-                    weight = (gate_w if d < deltas else up_w)[slot, j]
-                    columns = slice((d % deltas) * cw, (d % deltas + 1) * cw)
-                    rows = xline[d, :, mine, :].reshape(PLANE * group, cw)
-                    term = dot_t(rows, weight[:, columns])
-                    total = term if total is None else total + term
-                packed_line[c, :, mine, :] = total.astype(BF).reshape(PLANE, group, cw)
-            for b in (6, 7, 2, 4, 3, 5, 1):
-                give(c, b).start()
-            keep(c).start()
+    def produce(c):
+        slot = lax.rem(c, 2)
+
+        @pl.when(c + 1 < returns)
+        def _():
+            for load in first_loads(c + 1, 1 - slot):
+                load.start()
+
+        for load in first_loads(c, slot):
+            load.wait()
+        for j in range(owned):
+            mine = slice(j * group, (j + 1) * group)
+            total = None
+            for d in range(2 * deltas):
+                weight = gate_w if d < deltas else up_w
+                columns = slice((d % deltas) * cw, (d % deltas + 1) * cw)
+                rows = xline[d, :, mine, :].reshape(PLANE * group, cw)
+                term = dot_t(rows, weight[slot, j, :, columns])
+                total = term if total is None else total + term
+            packed_line[c, :, mine, :] = total.astype(BF).reshape(PLANE, group, cw)
+        for b in (2, 4, 6, 3, 5, 7, 1):
+            give(c, b).start()
+        keep(c).start()
 
     own = pl.ds(pl.multiple_of(z * tok, tok), tok)
 
-    @pl.loop(0, returns)
-    def _(c):
+    def merge(c):
         keep(c).wait()
         for b in range(1, PLANE):
             other = flipped(r, b)
@@ -603,8 +622,8 @@
             ).wait_recv()
         rows = rrecv[c].reshape(slots, cw)
         total = dot(mix_high[...], rows) + dot(mix_low[...], rows)
-        zsend[c] = total.astype(BF).reshape(planes, tok, cw)
-        for k in range(planes - 1, 0, -1):
+        zbuf[c] = total.astype(BF).reshape(planes, tok, cw)
+        for k in range(1, planes):
             home(c, k).start()
         columns = pl.ds(pl.multiple_of(c * cw, cw), cw)
         out_ref[:, columns] = dot(mix_high[own, :], rows) + dot(mix_low[own, :], rows)
@@ -630,8 +649,7 @@
             for k in range(1, planes):
                 home_gate(k).start()
 
-    @pl.loop(0, returns)
-    def _(c):
+    def finish(c):
         columns = pl.ds(pl.multiple_of(c * cw, cw), cw)
         total = out_ref[:, columns]
         for k in range(1, planes):
@@ -642,6 +660,20 @@
             ).wait_recv()
             total = total + zrecv[c, slot].astype(F32)
         out_ref[:, columns] = total
+
+    @pl.loop(0, returns + BEHIND + LAST)
+    def _(t):
+        @pl.when(t < returns)
+        def _():
+            produce(t)
+
+        @pl.when((t >= BEHIND) & (t < returns + BEHIND))
+        def _():
+            merge(t - BEHIND)
+
+        @pl.when(t >= BEHIND + LAST)
+        def _():
+            finish(t - BEHIND - LAST)
 
     total = zgsend[z]
     for k in range(1, planes):
@@ -658,17 +690,11 @@
     for k in range(1, planes):
         straight(*line_ranks, k).wait_send()
         straight(*line_amounts, k).wait_send()
-        first_straight(k).wait_send()
     for b in range(1, PLANE):
         ranks_hop(b).wait_send()
         give_gate(b).wait_send()
     for k in range(1, planes):
         home_gate(k).wait_send()
-
-    @pl.loop(1, 3 * supers)
-    def _(a):
-        for e in range(len(edges)):
-            line_hop(*data, (a,), e).wait_send()
 
     @pl.loop(0, supers)
     def _(s):
@@ -726,6 +752,7 @@
             pltpu.VMEM((owned, rows, ff), F32),
             pltpu.VMEM((owned, rows, ff), F32),
             pltpu.VMEM((owned, rows, ff), F32),
+            pltpu.VMEM((owned, rows, ff), F32),
             pltpu.VMEM((2, owned, cw, ff), BF),
             pltpu.VMEM((2, owned, cw, ff), BF),
             pltpu.VMEM((2, owned, ff, cw), BF),
@@ -735,7 +762,6 @@
             pltpu.VMEM((planes * tok, slots), BF),
             pltpu.VMEM((planes * tok, slots), BF),
             pltpu.VMEM((planes * tok, slots), BF),
-            pltpu.VMEM((half, planes, tok, cw), BF),
             pltpu.VMEM((half, planes, tok, cw), BF),
             pltpu.VMEM((planes, tok, LANES), F32),
             pltpu.VMEM((planes, tok, LANES), F32),
@@ -766,7 +792,7 @@
             dma((planes,)),
         ],
         compiler_params=pltpu.CompilerParams(
-            collective_id=0, has_side_effects=True, vmem_limit_bytes=63 * 2**20
+            collective_id=0, has_side_effects=True, vmem_limit_bytes=62 * 2**20
         ),
     )(tokens, cotangent, weights, ids, gate_weight, up_weight, down_weight)
 

time: 201 us -> 198 us (0.985)
    pallas_call x1, Pallas kernels: 196 us -> 194 us  [fused(): pl.pallas_call(functools.partial(fused_kernel, planes, cap, ring, 5), out...]
where the time goes in v2:
time: 198 us
  Pallas kernels  194 us (98%)
  local copies, waits for them, and re-layouts  3.57 us (2%)
    pallas_call x1, Pallas kernels, fused(): pl.pallas_call(functools.partial(fused_kernel, planes, cap, ring, 5), out...  194 us

profile of v2, /device:TPU:0, one launch (start us, length us, event | category | flops | bytes accessed | tf_op | source)
XLA Modules:
  0.0 198.0 jit_solution(18011866712264849900)
XLA Ops:
  0.6 193.8 %shard_map.86 = (f32[128,2048]{1,0:T(8,128)}, f32[8,128]{1,0:T(8,128)}) custom-call(bf16[128,2048]{1,0:T(8,128)(2,1)} %tokens_ref.1, bf16[128,2048]{1,0:T(8,128)(2,1)} %cotangent_ref.1, f32[8,128]{1,0:T(8,128)} %bitcast.3, s32[8,128]{1,0:T(8,128)} %bitcast.4, bf16[2,2048,768]{2,1,0:T(8,128)(2,1)} %gate_hbm.1, bf16[2,2048,768]{2,1,0:T(8,128)(2,1)} %up_hbm.1, ...), custom_call_target="tpu_custom_call" | custom-call | tf_op jit(solution)/shard_map/pallas_call | solution.py:731
  194.5 2.3 %copy.11 = f32[128,2048]{1,0:T(8,128)} copy(f32[128,2048]{1,0:T(8,128)} %get-tuple-element.8) | data formatting | bytes 2097152
  196.8 1.3 copy.12
